TPU v7x, 512 devices: a whole 4x8x8 slice. The times are simulated.
512 devices in a mesh: tile: 64 (over z, y), scan: 8 (over x, core).
Axes of the slice: x: 4, y: 8, z: 8, core: 2. Of those that a mesh axis runs over, the one named last changes fastest.
Arguments:
- object_real: float32 [3, 64, 128, 128], P(None, 'tile'), may hold values from 0.5 to 1.5
- object_imag: float32 [3, 64, 128, 128], P(None, 'tile'), may hold values from -1 to 1
- probe_modes: float32 [2, 2, 128, 128], replicated, may hold values from -6 to 6
- measured: float32 [64, 8, 1, 128, 128], P('tile', 'scan'), may hold values from 1 to 6
- offsets: int32 [64, 8, 1, 2], P('tile', 'scan'), may hold values from 0 to 127
- live: int32 [64, 8, 1], P('tile', 'scan'), may hold values 0 or 1
Outputs:
- object_real_out: float32 [3, 64, 128, 128], P(None, 'tile')
- object_imag_out: float32 [3, 64, 128, 128], P(None, 'tile')
- probe_out: float32 [2, 2, 128, 128], replicated
All inputs are finite; a program needn't handle non-finite values. No bound on the sum of `live` on one device may be relied on, other than what follows from the above.
Results may differ from a plain program's by a relative error of at most 0.0003.
Values sent between devices are 32-bit elements; how exact they have to be, the bound alone decides.
No kernel may reach another device: no remote copies, remote signals or barrier semaphores. Data moves between devices by JAX's collectives and lax.ppermute only.
A program may use at most 64 MiB of HBM per device.

v0:
```python
import math
import jax
import jax.numpy as jnp
from jax import lax
from jax.sharding import PartitionSpec as P

GRID = 8
ITERS = 2
object_rate = 0.008
probe_rate = 0.03


def shifted(shard, axis, by):
    size = lax.axis_size(axis)
    return lax.ppermute(shard, axis, [(i, (i + by) % size) for i in range(size)])


def make_tables(pattern_side):
    positions = lax.iota(jnp.int32, pattern_side)
    product = positions[:, None] * positions[None, :] % pattern_side
    angles = 2.0 * math.pi / pattern_side * product.astype(jnp.float32)
    scaling = 1.0 / math.sqrt(pattern_side)
    frequency = jnp.where(
        positions < pattern_side // 2, positions, positions - pattern_side
    ).astype(jnp.float32)
    phases = (
        -4.0
        * math.pi
        * (frequency[:, None] ** 2 + frequency[None, :] ** 2)
        / (pattern_side * pattern_side)
    )
    return (jnp.cos(angles) * scaling, jnp.sin(angles) * scaling, jnp.cos(phases), jnp.sin(phases))


def from_left(matrix, values):
    return jnp.einsum("jk,mkl->mjl", matrix, values, precision=lax.Precision.HIGHEST)


def from_right(values, matrix):
    return jnp.einsum("mjk,kl->mjl", values, matrix, precision=lax.Precision.HIGHEST)


def transform(part_real, part_imag, tables, sign):
    cosine, sine_table = (tables[0], tables[1])
    left_real = from_left(cosine, part_real) + sign * from_left(sine_table, part_imag)
    left_imag = from_left(cosine, part_imag) - sign * from_left(sine_table, part_real)
    out_real = from_right(left_real, cosine) + sign * from_right(left_imag, sine_table)
    out_imag = from_right(left_imag, cosine) - sign * from_right(left_real, sine_table)
    return (out_real, out_imag)


def slot_loss(patch_cells, mode_values, target, weight, tables):
    depth_count = patch_cells.shape[1]
    wave_real, wave_imag = (mode_values[:, 0], mode_values[:, 1])
    for depth_index in range(depth_count):
        cell_real = patch_cells[0, depth_index]
        cell_imag = patch_cells[1, depth_index]
        wave_real, wave_imag = (
            wave_real * cell_real - wave_imag * cell_imag,
            wave_real * cell_imag + wave_imag * cell_real,
        )
        if depth_index < depth_count - 1:
            freq_real, freq_imag = transform(wave_real, wave_imag, tables, 1.0)
            kern_real, kern_imag = (tables[2], tables[3])
            freq_real, freq_imag = (
                freq_real * kern_real - freq_imag * kern_imag,
                freq_real * kern_imag + freq_imag * kern_real,
            )
            wave_real, wave_imag = transform(freq_real, freq_imag, tables, -1.0)
    far_real, far_imag = transform(wave_real, wave_imag, tables, 1.0)
    intensity = jnp.sum(far_real**2 + far_imag**2, axis=0)
    return 0.5 * weight * jnp.sum((intensity - target) ** 2)


def local(object_real, object_imag, probe_modes, measured, offsets, live):
    slices = object_real.shape[0]
    block_side = object_real.shape[2]
    pattern_side = probe_modes.shape[2]
    slot_count = measured.shape[2]
    tile_count = lax.axis_size("tile")
    group_count = lax.axis_size("scan")
    tables = make_tables(pattern_side)
    anchor = jnp.zeros((), jnp.int32)
    obj_state = jnp.stack([object_real[:, 0], object_imag[:, 0]])
    for iteration in range(ITERS):
        right_part = shifted(obj_state, "tile", -1)
        below_part = shifted(obj_state, "tile", -GRID)
        corner_part = shifted(obj_state, "tile", -GRID - 1)
        upper_half = jnp.concatenate([obj_state, right_part], axis=-1)
        lower_half = jnp.concatenate([below_part, corner_part], axis=-1)
        canvas = jnp.concatenate([upper_half, lower_half], axis=-2)
        current_probe = probe_modes

        def visit_slot(slot_index, running):
            grad_canvas, grad_probe = running
            row_start = offsets[0, 0, slot_index, 0]
            col_start = offsets[0, 0, slot_index, 1]
            starts = (anchor, anchor, row_start, col_start)
            patch_cells = lax.dynamic_slice(canvas, starts, (2, slices, pattern_side, pattern_side))
            target = measured[0, 0, slot_index]
            weight = live[0, 0, slot_index].astype(jnp.float32)
            _, pullback = jax.vjp(
                lambda cell_values, mode_values: slot_loss(
                    cell_values, mode_values, target, weight, tables
                ),
                patch_cells,
                current_probe,
            )
            grad_patch, grad_modes = pullback(jnp.ones((), jnp.float32))
            current = lax.dynamic_slice(
                grad_canvas, starts, (2, slices, pattern_side, pattern_side)
            )
            grad_canvas = lax.dynamic_update_slice(grad_canvas, current + grad_patch, starts)
            return (grad_canvas, grad_probe + grad_modes)

        initial = (jnp.zeros_like(canvas), jnp.zeros_like(probe_modes))
        grad_canvas, grad_probe = lax.fori_loop(0, slot_count, visit_slot, initial)
        own_grad = grad_canvas[:, :, :block_side, :block_side]
        side_grad = grad_canvas[:, :, :block_side, block_side:]
        lower_grads = grad_canvas[:, :, block_side:, :]
        left_grad = shifted(side_grad, "tile", 1)
        above_grad = shifted(lower_grads[..., :block_side], "tile", GRID)
        diagonal_grad = shifted(lower_grads[..., block_side:], "tile", GRID + 1)
        grad_total = own_grad + above_grad + left_grad + diagonal_grad
        grad_total = lax.psum(grad_total, "scan")
        grad_probe = lax.psum(grad_probe, ("tile", "scan"))
        obj_state = obj_state - object_rate / (slot_count * group_count) * grad_total
        probe_modes = (
            probe_modes - probe_rate / (slot_count * tile_count * group_count) * grad_probe
        )
    return (obj_state[0][:, None], obj_state[1][:, None], probe_modes)


def solution(mesh):
    placed = (
        P(None, "tile", None, None),
        P(None, "tile", None, None),
        P(),
        P("tile", "scan", None, None, None),
        P("tile", "scan", None, None),
        P("tile", "scan", None),
    )
    return jax.shard_map(
        local,
        mesh=mesh,
        in_specs=placed,
        out_specs=(P(None, "tile", None, None), P(None, "tile", None, None), P()),
        check_vma=False,
    )
```

profile of v0, /device:TPU:8, one launch (start us, length us, event | category | flops | bytes accessed | tf_op | source)
XLA Modules:
  0.0 896.9 jit_solution(5106531731478892876)
XLA Ops:
  8.1 1.1 pad_maximum_fusion
  9.2 10.9 %collective-permute-start.1 = (f32[2,3,128,128]{3,2,1,0:T(8,128)S(1)}, f32[2,3,128,128]{3,2,1,0:T(8,128)S(1)}, u32[]{:S(2)}, u32[]{:S(2)}) collective-permute-start(f32[2,3,128,128]{3,2,1,0:T(8,128)S(1)} %pad_maximum_fusion), channel_id=1, source_target_pairs={{0,448},{8,456},{16,464},{24,472},{32,480},{40,488},{48,496},{56,5... | collective-permute-start | bytes 1179656 | tf_op jit(solution)/shard_map/ppermute | solution.py:15
  20.2 2.3 collective-permute-start.2
  22.5 5.4 collective-permute-start
  27.9 1.3 fusion.1195
  32.4 1.1 copy.315
  35.2 1.8 collective-permute-done.1
  36.9 4.1 collective-permute-done
  53.6 0.9 fusion.330
  66.8 0.7 fusion.311
  80.7 0.7 fusion.36
  87.6 4.1 dynamic_update_slice.8
  91.8 3.3 collective-permute-start.3
  95.2 3.2 collective-permute-start.5
  98.3 4.5 collective-permute-start.4
  102.8 2.2 collective-permute-done.3
  105.0 13.5 %collective-permute-done.5 = f32[2,3,128,128]{3,2,1,0:T(8,128)S(1)} collective-permute-done((f32[2,3,128,128]{3,2,1,0:T(8,128)S(1)}, f32[2,3,128,128]{3,2,1,0:T(8,128)S(1)}, u32[]{:S(2)}, u32[]{:S(2)}) %collective-permute-start.5) | collective-permute-done | bytes 393248 | tf_op jit(solution)/shard_map/ppermute | solution.py:15
  118.5 4.8 collective-permute-done.4
  123.3 0.8 fusion.70
  124.2 80.1 %all-reduce.21.cloned.1.call-done = f32[2,3,128,128]{3,2,1,0:T(8,128)} async-done(((f32[2,3,128,128]{3,2,1,0:T(8,128)}), f32[2,3,128,128]{3,2,1,0:T(8,128)}) %all-reduce.21.cloned.1.call-update) | async-done | bytes 393232 | tf_op jit(solution)/shard_map/psum | solution.py:125
  204.3 1.0 multiply_subtract_fusion.1
  205.4 5.8 collective-permute-start.8
  211.2 3.2 collective-permute-start.7
  214.4 5.5 collective-permute-start.6
  219.9 0.7 pad_add_fusion.3
  221.1 262.6 %all-reduce.23.cloned.1.call-done = f32[2,2,128,128]{2,3,0,1:T(8,128)} async-done(((f32[2,2,128,128]{2,3,0,1:T(8,128)}), f32[2,2,128,128]{2,3,0,1:T(8,128)}) %all-reduce.23.cloned.1.call-update) | async-done | bytes 262160 | tf_op jit(solution)/shard_map/psum | solution.py:126
  483.7 1.0 multiply_subtract_fusion.3
  489.8 0.6 convolution_multiply_fusion.6
  497.7 0.7 convolution_subtract_fusion.4
  505.8 0.6 fusion.21
  510.8 0.7 fusion.18
  524.7 0.8 fusion.4
  529.9 0.6 add_bitcast_fusion.1
  531.1 4.1 dynamic_update_slice.9
  535.2 1.0 fusion.1193
  536.3 3.5 collective-permute-start.9
  539.8 3.4 collective-permute-start.11
  543.2 2.8 collective-permute-start.10
  546.0 0.7 pad_add_fusion.2
  546.8 12.8 %collective-permute-done.9 = f32[2,3,128,128]{3,2,1,0:T(8,128)} collective-permute-done((f32[2,3,128,128]{3,2,1,0:T(8,128)}, f32[2,3,128,128]{3,2,1,0:T(8,128)}, u32[]{:S(2)}, u32[]{:S(2)}) %collective-permute-start.9) | collective-permute-done | bytes 393248 | tf_op jit(solution)/shard_map/ppermute | solution.py:15
  559.7 1.4 collective-permute-done.10
  561.1 2.1 fusion.68
  563.2 253.8 %all-reduce.27.cloned.1.call-done = f32[2,2,128,128]{2,3,0,1:T(8,128)} async-done(((f32[2,2,128,128]{2,3,0,1:T(8,128)}), f32[2,2,128,128]{2,3,0,1:T(8,128)}) %all-reduce.27.cloned.1.call-update) | async-done | bytes 262160 | tf_op jit(solution)/shard_map/psum | solution.py:126
  817.0 1.0 multiply_subtract_fusion.2
  818.0 0.8 copy.474
  818.8 68.3 %all-reduce.25.cloned.1.call-done = f32[2,3,128,128]{3,2,1,0:T(8,128)} async-done(((f32[2,3,128,128]{3,2,1,0:T(8,128)}), f32[2,3,128,128]{3,2,1,0:T(8,128)}) %all-reduce.25.cloned.1.call-update) | async-done | bytes 393232 | tf_op jit(solution)/shard_map/psum | solution.py:125
  887.1 1.1 multiply_subtract_fusion
  888.1 0.8 slice_bitcast_fusion
  (206 shorter events, 86.3 us)
Async XLA Ops:
  8.0 33.1 %copy-start.1 = (f32[3,1,128,128]{3,2,1,0:T(8,128)S(1)}, f32[3,1,128,128]{3,2,1,0:T(8,128)}, u32[]{:S(2)}) copy-start(f32[3,1,128,128]{3,2,1,0:T(8,128)} %param.7) | copy-start | bytes 589828
  8.0 33.1 %copy-start = (f32[3,1,128,128]{3,2,1,0:T(8,128)S(1)}, f32[3,1,128,128]{3,2,1,0:T(8,128)}, u32[]{:S(2)}) copy-start(f32[3,1,128,128]{3,2,1,0:T(8,128)} %param.6) | copy-start | bytes 589828
  8.0 196.3 %all-reduce.21.cloned.1.call-start = ((), (), s32[]{:S(2)}) async-start(), calls=%async_computation | async-start | bytes 786432 | tf_op jit(solution)/shard_map/psum | solution.py:125
  9.2 27.7 %collective-permute-start.1 = (f32[2,3,128,128]{3,2,1,0:T(8,128)S(1)}, f32[2,3,128,128]{3,2,1,0:T(8,128)S(1)}, u32[]{:S(2)}, u32[]{:S(2)}) collective-permute-start(f32[2,3,128,128]{3,2,1,0:T(8,128)S(1)} %pad_maximum_fusion), channel_id=1, source_target_pairs={{0,448},{8,456},{16,464},{24,472},{32,480},{40,488},{48,496},{56,5... | collective-permute-start | bytes 1179656 | tf_op jit(solution)/shard_map/ppermute | solution.py:15
  20.2 16.8 %collective-permute-start.2 = (f32[2,3,128,128]{3,2,1,0:T(8,128)S(1)}, f32[2,3,128,128]{3,2,1,0:T(8,128)S(1)}, u32[]{:S(2)}, u32[]{:S(2)}) collective-permute-start(f32[2,3,128,128]{3,2,1,0:T(8,128)S(1)} %pad_maximum_fusion), channel_id=1, source_target_pairs={{0,440},{8,448},{16,456},{24,464},{32,472},{40,480},{48,488},{56,4... | collective-permute-start | bytes 1179656 | tf_op jit(solution)/shard_map/ppermute | solution.py:15
  22.5 18.6 %collective-permute-start = (f32[2,3,128,128]{3,2,1,0:T(8,128)S(1)}, f32[2,3,128,128]{3,2,1,0:T(8,128)S(1)}, u32[]{:S(2)}, u32[]{:S(2)}) collective-permute-start(f32[2,3,128,128]{3,2,1,0:T(8,128)S(1)} %pad_maximum_fusion), channel_id=1, source_target_pairs={{0,504},{8,0},{16,8},{24,16},{32,24},{40,32},{48,40},{56,48},{64,5... | collective-permute-start | bytes 1179656 | tf_op jit(solution)/shard_map/ppermute | solution.py:15
  60.7 4.0 copy-start.3
  91.8 13.2 %collective-permute-start.3 = (f32[2,3,128,128]{3,2,1,0:T(8,128)S(1)}, f32[2,3,128,128]{3,2,1,0:T(8,128)S(1)}, u32[]{:S(2)}, u32[]{:S(2)}) collective-permute-start(f32[2,3,128,128]{3,2,1,0:T(8,128)S(1)} %get-tuple-element.121), channel_id=1, source_target_pairs={{0,64},{8,72},{16,80},{24,88},{32,96},{40,104},{48,112},{56,120},{... | collective-permute-start | bytes 1179656 | tf_op jit(solution)/shard_map/ppermute | solution.py:15
  95.2 23.4 %collective-permute-start.5 = (f32[2,3,128,128]{3,2,1,0:T(8,128)S(1)}, f32[2,3,128,128]{3,2,1,0:T(8,128)S(1)}, u32[]{:S(2)}, u32[]{:S(2)}) collective-permute-start(f32[2,3,128,128]{3,2,1,0:T(8,128)S(1)} %get-tuple-element.122), channel_id=1, source_target_pairs={{0,72},{8,80},{16,88},{24,96},{32,104},{40,112},{48,120},{56,128},... | collective-permute-start | bytes 1179656 | tf_op jit(solution)/shard_map/ppermute | solution.py:15
  98.3 25.0 %collective-permute-start.4 = (f32[2,3,128,128]{3,2,1,0:T(8,128)S(1)}, f32[2,3,128,128]{3,2,1,0:T(8,128)S(1)}, u32[]{:S(2)}, u32[]{:S(2)}) collective-permute-start(f32[2,3,128,128]{3,2,1,0:T(8,128)S(1)} %get-tuple-element.123), channel_id=1, source_target_pairs={{0,8},{8,16},{16,24},{24,32},{32,40},{40,48},{48,56},{56,64},{64,7... | collective-permute-start | bytes 1179656 | tf_op jit(solution)/shard_map/ppermute | solution.py:15
  124.2 359.5 %all-reduce.23.cloned.1.call-start = ((), (), s32[]{:S(2)}) async-start(), calls=%async_computation.1 | async-start | bytes 524288 | tf_op jit(solution)/shard_map/psum | solution.py:126
  205.4 279.3 %collective-permute-start.8 = (f32[2,3,128,128]{3,2,1,0:T(8,128)S(1)}, f32[2,3,128,128]{3,2,1,0:T(8,128)S(1)}, u32[]{:S(2)}, u32[]{:S(2)}) collective-permute-start(f32[2,3,128,128]{3,2,1,0:T(8,128)S(1)} %multiply_subtract_fusion.1), channel_id=1, source_target_pairs={{0,440},{8,448},{16,456},{24,464},{32,472},{40,480},{48,488},{56,4... | collective-permute-start | bytes 1179656 | tf_op jit(solution)/shard_map/ppermute | solution.py:15
  211.2 273.5 %collective-permute-start.7 = (f32[2,3,128,128]{3,2,1,0:T(8,128)S(1)}, f32[2,3,128,128]{3,2,1,0:T(8,128)S(1)}, u32[]{:S(2)}, u32[]{:S(2)}) collective-permute-start(f32[2,3,128,128]{3,2,1,0:T(8,128)S(1)} %multiply_subtract_fusion.1), channel_id=1, source_target_pairs={{0,448},{8,456},{16,464},{24,472},{32,480},{40,488},{48,496},{56,5... | collective-permute-start | bytes 1179656 | tf_op jit(solution)/shard_map/ppermute | solution.py:15
  214.4 270.3 %collective-permute-start.6 = (f32[2,3,128,128]{3,2,1,0:T(8,128)S(1)}, f32[2,3,128,128]{3,2,1,0:T(8,128)S(1)}, u32[]{:S(2)}, u32[]{:S(2)}) collective-permute-start(f32[2,3,128,128]{3,2,1,0:T(8,128)S(1)} %multiply_subtract_fusion.1), channel_id=1, source_target_pairs={{0,504},{8,0},{16,8},{24,16},{32,24},{40,32},{48,40},{56,48},{64,5... | collective-permute-start | bytes 1179656 | tf_op jit(solution)/shard_map/ppermute | solution.py:15
  220.6 596.3 %all-reduce.27.cloned.1.call-start = ((), (), s32[]{:S(2)}) async-start(), calls=%async_computation.3 | async-start | bytes 524288 | tf_op jit(solution)/shard_map/psum | solution.py:126
  536.3 23.4 %collective-permute-start.9 = (f32[2,3,128,128]{3,2,1,0:T(8,128)}, f32[2,3,128,128]{3,2,1,0:T(8,128)}, u32[]{:S(2)}, u32[]{:S(2)}) collective-permute-start(f32[2,3,128,128]{3,2,1,0:T(8,128)} %get-tuple-element.118), channel_id=1, source_target_pairs={{0,64},{8,72},{16,80},{24,88},{32,96},{40,104},{48,112},{56,120},{... | collective-permute-start | bytes 1179656 | tf_op jit(solution)/shard_map/ppermute | solution.py:15
  539.8 19.9 %collective-permute-start.11 = (f32[2,3,128,128]{3,2,1,0:T(8,128)}, f32[2,3,128,128]{3,2,1,0:T(8,128)}, u32[]{:S(2)}, u32[]{:S(2)}) collective-permute-start(f32[2,3,128,128]{3,2,1,0:T(8,128)} %get-tuple-element.119), channel_id=1, source_target_pairs={{0,72},{8,80},{16,88},{24,96},{32,104},{40,112},{48,120},{56,128},... | collective-permute-start | bytes 1179656 | tf_op jit(solution)/shard_map/ppermute | solution.py:15
  543.2 17.9 %collective-permute-start.10 = (f32[2,3,128,128]{3,2,1,0:T(8,128)S(1)}, f32[2,3,128,128]{3,2,1,0:T(8,128)}, u32[]{:S(2)}, u32[]{:S(2)}) collective-permute-start(f32[2,3,128,128]{3,2,1,0:T(8,128)S(1)} %get-tuple-element.120), channel_id=1, source_target_pairs={{0,8},{8,16},{16,24},{24,32},{32,40},{40,48},{48,56},{56,64},{64,7... | collective-permute-start | bytes 1179656 | tf_op jit(solution)/shard_map/ppermute | solution.py:15
  546.8 340.3 %copy-start.2 = (f32[2,3,128,128]{3,2,1,0:T(8,128)S(1)}, f32[2,3,128,128]{3,2,1,0:T(8,128)}, u32[]{:S(2)}) copy-start(f32[2,3,128,128]{3,2,1,0:T(8,128)} %all-reduce.21.cloned.1.call-done) | copy-start | bytes 1179652
  546.8 340.3 %all-reduce.25.cloned.1.call-start = ((), (), s32[]{:S(2)}) async-start(), calls=%async_computation.2 | async-start | bytes 786432 | tf_op jit(solution)/shard_map/psum | solution.py:125
Sparse Core Ops, SparseCore 0:
  124.3 79.9 all-reduce.20
Sparse Core Ops, SparseCore 1:
  220.7 262.9 all-reduce.22
  546.8 270.1 all-reduce.26
  819.3 67.7 all-reduce.24
where the time goes:
time: 906 us; the launch traced here: 897 us
  waiting for transfers between devices  706 us (78%)
  matrix products  88.9 us (10%)
  starting transfers between devices  54.4 us (6%)
  between operations  22.3 us (2%)
  local copies, waits for them, and re-layouts  14.7 us (2%)
  other arithmetic  11 us (1%)
    psum x2, waiting for transfers between devices, local(): grad_probe = lax.psum(grad_probe, ('tile', 'scan'))  516 us
    psum x2, waiting for transfers between devices, local(): grad_total = lax.psum(grad_total, 'scan')  148 us
    ppermute x12, starting transfers between devices, shifted(): lax.ppermute(shard, axis, [(i, (i + by) % size) for i in range(size)])  53.8 us
    dot_general x80, matrix products, from_left(): jnp.einsum('jk,mkl->mjl', matrix, values, precision=lax.Precision.HIGHEST)  44.9 us
    dot_general x80, matrix products, from_right(): jnp.einsum('mjk,kl->mjl', values, matrix, precision=lax.Precision.HIGHEST)  44 us
    ppermute x12, waiting for transfers between devices, shifted(): lax.ppermute(shard, axis, [(i, (i + by) % size) for i in range(size)])  40.7 us
  transfers between devices with their start and end apart: 16, of which 11 were waited for; matrix products, arithmetic and copies ran while one was open for 1% of the time, Pallas kernels for 0%

commit v1 on v0

--- a/solution.py
+++ b/solution.py
@@ -123,7 +123,8 @@
         diagonal_grad = shifted(lower_grads[..., block_side:], "tile", GRID + 1)
         grad_total = own_grad + above_grad + left_grad + diagonal_grad
         grad_total = lax.psum(grad_total, "scan")
-        grad_probe = lax.psum(grad_probe, ("tile", "scan"))
+        inner = lax.psum(grad_probe, "tile")
+        grad_probe = lax.psum(inner, "scan")
         obj_state = obj_state - object_rate / (slot_count * group_count) * grad_total
         probe_modes = (
             probe_modes - probe_rate / (slot_count * tile_count * group_count) * grad_probe

time: 906 us -> 685 us (0.76)
  waiting for transfers between devices: 706 us -> 485 us
    psum x2, waiting for transfers between devices: 516 us -> 291 us  [local(): inner = lax.psum(grad_probe, 'tile')]
    ppermute x12, waiting for transfers between devices: 40.7 us -> 50.6 us  [shifted(): lax.ppermute(shard, axis, [(i, (i + by) % size) for i in range(size)])]
  transfers between devices with their start and end apart: 16 -> 16, of which waited for: 11 -> 14; matrix products, arithmetic and copies ran while one was open for 1% -> 1% of each run, Pallas kernels for 0% -> 0%
where the time goes in v1:
time: 685 us; the launch traced here: 676 us
  waiting for transfers between devices  485 us (71%)
  matrix products  89 us (13%)
  starting transfers between devices  54.8 us (8%)
  between operations  20.4 us (3%)
  local copies, waits for them, and re-layouts  15.5 us (2%)
  other arithmetic  11.4 us (2%)
    psum x2, waiting for transfers between devices, local(): inner = lax.psum(grad_probe, 'tile')  291 us
    psum x2, waiting for transfers between devices, local(): grad_total = lax.psum(grad_total, 'scan')  143 us
    ppermute x12, starting transfers between devices, shifted(): lax.ppermute(shard, axis, [(i, (i + by) % size) for i in range(size)])  54.6 us
    ppermute x12, waiting for transfers between devices, shifted(): lax.ppermute(shard, axis, [(i, (i + by) % size) for i in range(size)])  50.6 us
    dot_general x80, matrix products, from_left(): jnp.einsum('jk,mkl->mjl', matrix, values, precision=lax.Precision.HIGHEST)  44.9 us
    dot_general x80, matrix products, from_right(): jnp.einsum('mjk,kl->mjl', values, matrix, precision=lax.Precision.HIGHEST)  44.1 us
  transfers between devices with their start and end apart: 16, of which 14 were waited for; matrix products, arithmetic and copies ran while one was open for 1% of the time, Pallas kernels for 0%

profile of v1, /device:TPU:8, one launch (start us, length us, event | category | flops | bytes accessed | tf_op | source)
XLA Modules:
  0.0 675.8 jit_solution(17537170591981041838)
XLA Ops:
  7.2 1.1 pad_maximum_fusion
  8.4 10.9 %collective-permute-start.1 = (f32[2,3,128,128]{3,2,1,0:T(8,128)S(1)}, f32[2,3,128,128]{3,2,1,0:T(8,128)S(1)}, u32[]{:S(2)}, u32[]{:S(2)}) collective-permute-start(f32[2,3,128,128]{3,2,1,0:T(8,128)S(1)} %pad_maximum_fusion), channel_id=1, source_target_pairs={{0,448},{8,456},{16,464},{24,472},{32,480},{40,488},{48,496},{56,5... | collective-permute-start | bytes 1179656 | tf_op jit(solution)/shard_map/ppermute | solution.py:15
  19.3 2.3 collective-permute-start.2
  21.7 5.4 collective-permute-start
  27.1 1.3 fusion.1195
  31.6 1.1 copy.315
  34.3 1.8 collective-permute-done.1
  36.1 4.1 collective-permute-done
  52.7 0.9 fusion.330
  66.0 0.7 fusion.311
  79.9 0.7 fusion.36
  86.8 4.1 dynamic_update_slice.8
  90.9 0.9 fusion.1194
  91.8 3.3 collective-permute-start.3
  95.1 3.2 collective-permute-start.5
  98.3 4.5 collective-permute-start.4
  102.8 0.7 pad_add_fusion.3
  103.6 1.7 collective-permute-done.3
  105.3 13.3 %collective-permute-done.5 = f32[2,3,128,128]{3,2,1,0:T(8,128)} collective-permute-done((f32[2,3,128,128]{3,2,1,0:T(8,128)S(1)}, f32[2,3,128,128]{3,2,1,0:T(8,128)}, u32[]{:S(2)}, u32[]{:S(2)}) %collective-permute-start.5) | collective-permute-done | bytes 393248 | tf_op jit(solution)/shard_map/ppermute | solution.py:15
  118.6 4.8 collective-permute-done.4
  123.4 2.1 fusion.70
  125.4 141.1 %all-reduce.23.cloned.1.call-done = f32[2,2,128,128]{2,3,0,1:T(8,128)} async-done(((f32[2,2,128,128]{2,3,0,1:T(8,128)}), f32[2,2,128,128]{2,3,0,1:T(8,128)}) %all-reduce.23.cloned.1.call-update) | async-done | bytes 262160 | tf_op jit(solution)/shard_map/psum | solution.py:126
  266.6 71.6 %all-reduce.29.cloned.1.call-done = (f32[2,3,128,128]{3,2,1,0:T(8,128)}, f32[2,2,128,128]{2,3,0,1:T(8,128)}) async-done(((f32[2,3,128,128]{3,2,1,0:T(8,128)}, f32[2,2,128,128]{2,3,0,1:T(8,128)}), (f32[2,3,128,128]{3,2,1,0:T(8,128)}, f32[2,2,128,128]{2,3,0,1:T(8,128)})) %all-reduce.29.cloned.1.call-update) | async-done | bytes 655376 | tf_op jit(solution)/shard_map/psum | solution.py:125
  338.2 1.0 multiply_subtract_fusion.1
  339.3 5.8 collective-permute-start.8
  345.1 3.2 collective-permute-start.7
  348.3 5.9 collective-permute-start.6
  354.2 1.0 multiply_subtract_fusion.3
  355.2 5.6 collective-permute-done.7
  360.8 1.1 collective-permute-done.6
  374.9 0.7 convolution_subtract_fusion.4
  388.0 0.7 fusion.18
  401.9 0.8 fusion.4
  408.3 4.1 dynamic_update_slice.9
  412.4 1.0 fusion.1193
  413.4 1.9 collective-permute-start.9
  415.3 3.8 collective-permute-start.11
  419.1 4.5 collective-permute-start.10
  423.6 0.7 pad_add_fusion.2
  424.4 3.3 collective-permute-done.9
  427.7 12.9 %collective-permute-done.11 = f32[2,3,128,128]{3,2,1,0:T(8,128)} collective-permute-done((f32[2,3,128,128]{3,2,1,0:T(8,128)}, f32[2,3,128,128]{3,2,1,0:T(8,128)}, u32[]{:S(2)}, u32[]{:S(2)}) %collective-permute-start.11) | collective-permute-done | bytes 393248 | tf_op jit(solution)/shard_map/ppermute | solution.py:15
  440.6 2.0 collective-permute-done.10
  442.6 2.0 fusion.68
  444.6 150.0 %all-reduce.25.cloned.1.call-done = f32[2,2,128,128]{2,3,0,1:T(8,128)} async-done(((f32[2,2,128,128]{2,3,0,1:T(8,128)}), f32[2,2,128,128]{2,3,0,1:T(8,128)}) %all-reduce.25.cloned.1.call-update) | async-done | bytes 262160 | tf_op jit(solution)/shard_map/psum | solution.py:126
  594.6 71.4 %all-reduce.27.cloned.1.call-done = (f32[2,3,128,128]{3,2,1,0:T(8,128)}, f32[2,2,128,128]{2,3,0,1:T(8,128)}) async-done(((f32[2,3,128,128]{3,2,1,0:T(8,128)}, f32[2,2,128,128]{2,3,0,1:T(8,128)}), (f32[2,3,128,128]{3,2,1,0:T(8,128)}, f32[2,2,128,128]{2,3,0,1:T(8,128)})) %all-reduce.27.cloned.1.call-update) | async-done | bytes 655376 | tf_op jit(solution)/shard_map/psum | solution.py:125
  666.0 1.1 multiply_subtract_fusion
  667.2 0.8 copy.474
  668.0 0.8 slice_bitcast_fusion
  (208 shorter events, 87.6 us)
Async XLA Ops:
  7.2 33.1 %copy-start.1 = (f32[3,1,128,128]{3,2,1,0:T(8,128)S(1)}, f32[3,1,128,128]{3,2,1,0:T(8,128)}, u32[]{:S(2)}) copy-start(f32[3,1,128,128]{3,2,1,0:T(8,128)} %param.7) | copy-start | bytes 589828
  7.2 33.1 %copy-start = (f32[3,1,128,128]{3,2,1,0:T(8,128)S(1)}, f32[3,1,128,128]{3,2,1,0:T(8,128)}, u32[]{:S(2)}) copy-start(f32[3,1,128,128]{3,2,1,0:T(8,128)} %param.6) | copy-start | bytes 589828
  7.2 259.4 %all-reduce.23.cloned.1.call-start = ((), (), s32[]{:S(2)}) async-start(), calls=%async_computation | async-start | bytes 524288 | tf_op jit(solution)/shard_map/psum | solution.py:126
  8.4 27.7 %collective-permute-start.1 = (f32[2,3,128,128]{3,2,1,0:T(8,128)S(1)}, f32[2,3,128,128]{3,2,1,0:T(8,128)S(1)}, u32[]{:S(2)}, u32[]{:S(2)}) collective-permute-start(f32[2,3,128,128]{3,2,1,0:T(8,128)S(1)} %pad_maximum_fusion), channel_id=1, source_target_pairs={{0,448},{8,456},{16,464},{24,472},{32,480},{40,488},{48,496},{56,5... | collective-permute-start | bytes 1179656 | tf_op jit(solution)/shard_map/ppermute | solution.py:15
  19.3 16.8 %collective-permute-start.2 = (f32[2,3,128,128]{3,2,1,0:T(8,128)S(1)}, f32[2,3,128,128]{3,2,1,0:T(8,128)S(1)}, u32[]{:S(2)}, u32[]{:S(2)}) collective-permute-start(f32[2,3,128,128]{3,2,1,0:T(8,128)S(1)} %pad_maximum_fusion), channel_id=1, source_target_pairs={{0,440},{8,448},{16,456},{24,464},{32,472},{40,480},{48,488},{56,4... | collective-permute-start | bytes 1179656 | tf_op jit(solution)/shard_map/ppermute | solution.py:15
  21.7 18.6 %collective-permute-start = (f32[2,3,128,128]{3,2,1,0:T(8,128)S(1)}, f32[2,3,128,128]{3,2,1,0:T(8,128)S(1)}, u32[]{:S(2)}, u32[]{:S(2)}) collective-permute-start(f32[2,3,128,128]{3,2,1,0:T(8,128)S(1)} %pad_maximum_fusion), channel_id=1, source_target_pairs={{0,504},{8,0},{16,8},{24,16},{32,24},{40,32},{48,40},{56,48},{64,5... | collective-permute-start | bytes 1179656 | tf_op jit(solution)/shard_map/ppermute | solution.py:15
  59.9 4.0 copy-start.4
  91.8 13.5 %collective-permute-start.3 = (f32[2,3,128,128]{3,2,1,0:T(8,128)}, f32[2,3,128,128]{3,2,1,0:T(8,128)}, u32[]{:S(2)}, u32[]{:S(2)}) collective-permute-start(f32[2,3,128,128]{3,2,1,0:T(8,128)} %get-tuple-element.125), channel_id=1, source_target_pairs={{0,64},{8,72},{16,80},{24,88},{32,96},{40,104},{48,112},{56,120},{... | collective-permute-start | bytes 1179656 | tf_op jit(solution)/shard_map/ppermute | solution.py:15
  95.1 23.5 %collective-permute-start.5 = (f32[2,3,128,128]{3,2,1,0:T(8,128)S(1)}, f32[2,3,128,128]{3,2,1,0:T(8,128)}, u32[]{:S(2)}, u32[]{:S(2)}) collective-permute-start(f32[2,3,128,128]{3,2,1,0:T(8,128)S(1)} %get-tuple-element.126), channel_id=1, source_target_pairs={{0,72},{8,80},{16,88},{24,96},{32,104},{40,112},{48,120},{56,128},... | collective-permute-start | bytes 1179656 | tf_op jit(solution)/shard_map/ppermute | solution.py:15
  98.3 25.1 %collective-permute-start.4 = (f32[2,3,128,128]{3,2,1,0:T(8,128)S(1)}, f32[2,3,128,128]{3,2,1,0:T(8,128)}, u32[]{:S(2)}, u32[]{:S(2)}) collective-permute-start(f32[2,3,128,128]{3,2,1,0:T(8,128)S(1)} %get-tuple-element.127), channel_id=1, source_target_pairs={{0,8},{8,16},{16,24},{24,32},{32,40},{40,48},{48,56},{56,64},{64,7... | collective-permute-start | bytes 1179656 | tf_op jit(solution)/shard_map/ppermute | solution.py:15
  103.5 234.7 %all-reduce.29.cloned.1.call-start = ((), (), s32[]{:S(2)}) async-start(), calls=%async_computation.3 | async-start | bytes 1310720 | tf_op jit(solution)/shard_map/psum | solution.py:125
  266.6 328.0 %all-reduce.25.cloned.1.call-start = ((), (), s32[]{:S(2)}) async-start(), calls=%async_computation.1 | async-start | bytes 524288 | tf_op jit(solution)/shard_map/psum | solution.py:126
  339.3 15.9 %collective-permute-start.8 = (f32[2,3,128,128]{3,2,1,0:T(8,128)S(1)}, f32[2,3,128,128]{3,2,1,0:T(8,128)S(1)}, u32[]{:S(2)}, u32[]{:S(2)}) collective-permute-start(f32[2,3,128,128]{3,2,1,0:T(8,128)S(1)} %multiply_subtract_fusion.1), channel_id=1, source_target_pairs={{0,440},{8,448},{16,456},{24,464},{32,472},{40,480},{48,488},{56,4... | collective-permute-start | bytes 1179656 | tf_op jit(solution)/shard_map/ppermute | solution.py:15
  345.1 15.6 %collective-permute-start.7 = (f32[2,3,128,128]{3,2,1,0:T(8,128)S(1)}, f32[2,3,128,128]{3,2,1,0:T(8,128)S(1)}, u32[]{:S(2)}, u32[]{:S(2)}) collective-permute-start(f32[2,3,128,128]{3,2,1,0:T(8,128)S(1)} %multiply_subtract_fusion.1), channel_id=1, source_target_pairs={{0,448},{8,456},{16,464},{24,472},{32,480},{40,488},{48,496},{56,5... | collective-permute-start | bytes 1179656 | tf_op jit(solution)/shard_map/ppermute | solution.py:15
  348.3 13.5 %collective-permute-start.6 = (f32[2,3,128,128]{3,2,1,0:T(8,128)S(1)}, f32[2,3,128,128]{3,2,1,0:T(8,128)S(1)}, u32[]{:S(2)}, u32[]{:S(2)}) collective-permute-start(f32[2,3,128,128]{3,2,1,0:T(8,128)S(1)} %multiply_subtract_fusion.1), channel_id=1, source_target_pairs={{0,504},{8,0},{16,8},{24,16},{32,24},{40,32},{48,40},{56,48},{64,5... | collective-permute-start | bytes 1179656 | tf_op jit(solution)/shard_map/ppermute | solution.py:15
  413.4 14.3 %collective-permute-start.9 = (f32[2,3,128,128]{3,2,1,0:T(8,128)}, f32[2,3,128,128]{3,2,1,0:T(8,128)}, u32[]{:S(2)}, u32[]{:S(2)}) collective-permute-start(f32[2,3,128,128]{3,2,1,0:T(8,128)} %get-tuple-element.122), channel_id=1, source_target_pairs={{0,64},{8,72},{16,80},{24,88},{32,96},{40,104},{48,112},{56,120},{... | collective-permute-start | bytes 1179656 | tf_op jit(solution)/shard_map/ppermute | solution.py:15
  415.3 25.2 %collective-permute-start.11 = (f32[2,3,128,128]{3,2,1,0:T(8,128)}, f32[2,3,128,128]{3,2,1,0:T(8,128)}, u32[]{:S(2)}, u32[]{:S(2)}) collective-permute-start(f32[2,3,128,128]{3,2,1,0:T(8,128)} %get-tuple-element.123), channel_id=1, source_target_pairs={{0,72},{8,80},{16,88},{24,96},{32,104},{40,112},{48,120},{56,128},... | collective-permute-start | bytes 1179656 | tf_op jit(solution)/shard_map/ppermute | solution.py:15
  419.1 23.5 %collective-permute-start.10 = (f32[2,3,128,128]{3,2,1,0:T(8,128)S(1)}, f32[2,3,128,128]{3,2,1,0:T(8,128)}, u32[]{:S(2)}, u32[]{:S(2)}) collective-permute-start(f32[2,3,128,128]{3,2,1,0:T(8,128)S(1)} %get-tuple-element.124), channel_id=1, source_target_pairs={{0,8},{8,16},{16,24},{24,32},{32,40},{40,48},{48,56},{56,64},{64,7... | collective-permute-start | bytes 1179656 | tf_op jit(solution)/shard_map/ppermute | solution.py:15
  424.3 241.7 %copy-start.2 = (f32[2,3,128,128]{3,2,1,0:T(8,128)S(1)}, f32[2,3,128,128]{3,2,1,0:T(8,128)}, u32[]{:S(2)}) copy-start(f32[2,3,128,128]{3,2,1,0:T(8,128)} %get-tuple-element.120) | copy-start | bytes 1179652
  424.3 241.7 %all-reduce.27.cloned.1.call-start = ((), (), s32[]{:S(2)}) async-start(), calls=%async_computation.2 | async-start | bytes 1310720 | tf_op jit(solution)/shard_map/psum | solution.py:125
  666.0 1.1 copy-start.3
Sparse Core Ops, SparseCore 0:
  103.6 162.8 all-reduce.22
  269.2 68.9 all-reduce.28
  424.4 170.1 all-reduce.24
  597.0 68.9 all-reduce.26
